TPU v7x, 512 devices: a whole 4x4x16 slice. The times are simulated.
512 devices in a mesh: row: 64 (over x, y, z_hi, core), col: 8 (over z_lo).
Axes of the slice: x: 4, y: 4, z: 16 (z_hi: 2, z_lo: 8; z = z_hi * 8 + z_lo), core: 2. Of those that a mesh axis runs over, the one named last changes fastest.
Arguments:
- inputs: bfloat16 [256, 1024, 256], P('row', 'col'), may hold values from -6 to 6
- preactivation: bfloat16 [256, 1024, 256], P('row', 'col'), may hold values from -6 to 6
- cotangent: bfloat16 [256, 1024, 256], P('row', 'col'), may hold values from -6 to 6
- spectral: bfloat16 [2, 128, 64, 5, 1024], P(None, 'row', 'col'), may hold values from -2 to 2
- bypass: bfloat16 [32, 32], replicated, may hold values from -1 to 1
Outputs:
- grad_inputs: bfloat16 [256, 1024, 256], P('row', 'col')
- grad_spectral: float32 [2, 128, 64, 5, 1024], P(None, 'row', 'col')
- grad_bypass: float32 [32, 32], replicated
All inputs are finite; a program needn't handle non-finite values.
Results may differ from a plain program's by a relative error of at most 0.022.
Values may be sent and summed in bfloat16 or wider, within the bound.
A program may use at most 64 MiB of HBM per device.

v0:
```python
import math
import jax
import jax.numpy as jnp
from jax import lax
from jax.sharding import PartitionSpec as P

exact_mode = lax.Precision.HIGHEST


def counting(length):
    return jnp.arange(length, dtype=jnp.int32)


def kept_freq(slot_index, keep_count):
    return jnp.where(slot_index < keep_count // 2, slot_index, slot_index - keep_count)


def phase_table(outer_index, inner_index, length, direction):
    turn_count = jnp.mod(outer_index[:, None] * inner_index[None, :], length)
    angles = turn_count.astype(jnp.float32) * (2.0 * math.pi / length)
    cosine = jnp.cos(angles)
    sine_part = direction * jnp.sin(angles)
    top_rows = jnp.stack([cosine, -sine_part], axis=1)
    low_rows = jnp.stack([sine_part, cosine], axis=1)
    return jnp.stack([top_rows, low_rows], axis=0)


def time_forward(step_count, time_modes):
    turn_count = jnp.mod(counting(step_count)[:, None] * counting(time_modes)[None, :], step_count)
    angles = turn_count.astype(jnp.float32) * (2.0 * math.pi / step_count)
    return jnp.stack([jnp.cos(angles), -jnp.sin(angles)], axis=1)


def time_inverse(step_count, time_modes):
    turn_count = jnp.mod(counting(time_modes)[:, None] * counting(step_count)[None, :], step_count)
    angles = turn_count.astype(jnp.float32) * (2.0 * math.pi / step_count)
    return jnp.stack([jnp.cos(angles), -jnp.sin(angles)], axis=0)


def gelu_slope(values):
    normal_cdf = 0.5 * (1.0 + lax.erf(values * (1.0 / math.sqrt(2.0))))
    density = jnp.exp(-0.5 * values * values) * (1.0 / math.sqrt(2.0 * math.pi))
    return normal_cdf + values * density


def mix_modes(modes_in, modes_grad, weight, factor):
    in_real = modes_in[:, 0]
    in_imag = modes_in[:, 1]
    grad_real = modes_grad[:, 0]
    grad_imag = modes_grad[:, 1]
    real_part = factor * (
        in_real[..., :, None] * grad_real[..., None, :]
        + in_imag[..., :, None] * grad_imag[..., None, :]
    )
    imag_part = factor * (
        in_real[..., :, None] * grad_imag[..., None, :]
        - in_imag[..., :, None] * grad_real[..., None, :]
    )
    weight_grad = jnp.stack([real_part, imag_part], axis=0)
    w_real = weight[0]
    w_imag = weight[1]
    back_real = factor * (
        jnp.einsum("kyscd,kysd->kysc", w_real, grad_real, precision=exact_mode)
        + jnp.einsum("kyscd,kysd->kysc", w_imag, grad_imag, precision=exact_mode)
    )
    back_imag = factor * (
        jnp.einsum("kyscd,kysd->kysc", w_real, grad_imag, precision=exact_mode)
        - jnp.einsum("kyscd,kysd->kysc", w_imag, grad_real, precision=exact_mode)
    )
    return (weight_grad, jnp.stack([back_real, back_imag], axis=1))


def local(inputs, preactivation, cotangent, spectral, bypass):
    row_count, col_count, packed = inputs.shape
    chan_count = bypass.shape[0]
    step_count = packed // chan_count
    time_modes = spectral.shape[3]
    owned_row_modes = spectral.shape[1]
    owned_col_modes = spectral.shape[2]
    row_parts = lax.axis_size("row")
    col_parts = lax.axis_size("col")
    row_modes = owned_row_modes * row_parts
    col_modes = owned_col_modes * col_parts
    total_x = row_count * row_parts
    total_y = col_count * col_parts
    factor = 1.0 / math.sqrt(
        float(total_x * total_y * step_count * row_modes * col_modes * time_modes)
    )
    row_start = lax.axis_index("row") * row_count
    col_start = lax.axis_index("col") * col_count
    mode_width = owned_col_modes * time_modes * chan_count
    slopes = gelu_slope(preactivation.astype(jnp.float32))
    pre_grad = (cotangent.astype(jnp.float32) * slopes).astype(jnp.bfloat16)
    flat_inputs = inputs.reshape(-1, chan_count)
    flat_grad = pre_grad.reshape(-1, chan_count)
    local_bypass = jnp.einsum(
        "nc,nd->cd", flat_inputs, flat_grad, preferred_element_type=jnp.float32
    )
    bypass_total = lax.psum(local_bypass, ("row", "col"))
    grad_bypass = bypass_total * (1.0 / math.sqrt(float(total_x * total_y * step_count)))
    forward_t = time_forward(step_count, time_modes)
    col_table = phase_table(counting(col_modes), col_start + counting(col_count), total_y, -1.0)

    def column_terms(field):
        cube_view = field.astype(jnp.float32).reshape(row_count, col_count, step_count, chan_count)
        in_time = jnp.einsum("rytc,tqs->ryqsc", cube_view, forward_t, precision=exact_mode)
        return jnp.einsum("akpy,rypsc->raksc", col_table, in_time, precision=exact_mode)

    col_in, col_grad = (
        lax.psum_scatter(
            column_terms(inputs).astype(jnp.bfloat16), "col", scatter_dimension=2, tiled=True
        ).astype(jnp.float32),
        lax.psum_scatter(
            column_terms(pre_grad).astype(jnp.bfloat16), "col", scatter_dimension=2, tiled=True
        ).astype(jnp.float32),
    )
    flat_in = col_in.reshape(row_count, 2, mode_width)
    flat_cols = col_grad.reshape(row_count, 2, mode_width)
    stacked = jnp.stack([flat_in, flat_cols], axis=2)
    frequencies = kept_freq(counting(owned_row_modes * lax.axis_size("row")), row_modes)
    phases = phase_table(frequencies, row_start + counting(row_count), total_x, -1.0)
    owned_modes = lax.psum_scatter(
        jnp.einsum("akpr,rpbm->kabm", phases, stacked, precision=exact_mode),
        "row",
        scatter_dimension=0,
        tiled=True,
    )
    modes_in = owned_modes[:, :, 0]
    modes_grad = owned_modes[:, :, 1]
    mode_shape = (owned_row_modes, 2, owned_col_modes, time_modes, chan_count)
    weight = spectral.astype(jnp.float32).reshape(
        2, owned_row_modes, owned_col_modes, time_modes, chan_count, chan_count
    )
    weight_grad, back_modes = mix_modes(
        modes_in.reshape(mode_shape), modes_grad.reshape(mode_shape), weight, factor
    )
    grad_spectral = weight_grad.reshape(spectral.shape)
    flat_back = back_modes.reshape(owned_row_modes, 2, mode_width)
    mode_piece = lax.all_gather(flat_back, "row", axis=0, tiled=True)
    span_count = mode_piece.shape[0]
    frequencies = kept_freq(counting(span_count), row_modes)
    phases = phase_table(row_start + counting(row_count), frequencies, total_x, 1.0)
    rows_back = jnp.einsum("axpk,kpm->xam", phases, mode_piece, precision=exact_mode)
    rows_view = rows_back.reshape(row_count, 2, owned_col_modes, time_modes, chan_count)
    col_piece = lax.all_gather(rows_view.astype(jnp.bfloat16), "col", axis=2, tiled=True).astype(
        jnp.float32
    )
    span_count = col_piece.shape[2]
    phases = phase_table(col_start + counting(col_count), counting(span_count), total_y, 1.0)
    cells_y = jnp.zeros(
        (row_count, col_count, 2, time_modes, chan_count), jnp.float32
    ) + jnp.einsum("aypk,rpksc->ryasc", phases, col_piece, precision=exact_mode)
    kernel_grad = jnp.einsum(
        "ryasc,ast->rytc", cells_y, time_inverse(step_count, time_modes), precision=exact_mode
    )
    bypass_grad = jnp.einsum("nd,cd->nc", flat_grad, bypass, preferred_element_type=jnp.float32)
    total_grad = kernel_grad.reshape(-1, chan_count) + bypass_grad
    grad_inputs = total_grad.reshape(inputs.shape).astype(jnp.bfloat16)
    return (grad_inputs, grad_spectral, grad_bypass)


def solution(mesh):
    return jax.shard_map(
        local,
        mesh=mesh,
        in_specs=(
            P("row", "col", None),
            P("row", "col", None),
            P("row", "col", None),
            P(None, "row", "col", None, None),
            P(),
        ),
        out_specs=(P("row", "col", None), P(None, "row", "col", None, None), P()),
        check_vma=False,
    )
```

profile of v0, /device:TPU:4, one launch (start us, length us, event | category | flops | bytes accessed | tf_op | source)
XLA Modules:
  0.0 1429.1 jit_solution(1506078009365955725)
XLA Ops:
  7.5 1.1 copy.63
  8.6 1.1 copy.64
  10.6 0.7 fusion.7
  11.3 1.2 copy.67
  13.3 0.7 fusion.8
  14.0 1.2 copy.61
  15.3 1.3 dynamic-slice
  17.3 133.3 %all-reduce.9.cloned.1.call-done = (bf16[4,2,64,5,32]{4,0,3,1,2:T(4,128)(2,1)}, bf16[4,2,64,5,32]{4,0,3,1,2:T(4,128)(2,1)}) async-done(((bf16[4,2,64,5,32]{4,0,3,1,2:T(4,128)(2,1)}, bf16[4,2,64,5,32]{4,0,3,1,2:T(4,128)(2,1)}), (bf16[4,2,64,5,32]{4,0,3,1,2:T(4,128)(2,1)}, bf16[4,2,64,5,32]{4,0,3,1,2:T(4,128)(2,1)})) %all-reduce.9.cloned.1.call-update) | async-done | bytes 327696
  150.6 0.9 constant_dynamic-slice_fusion.1
  151.7 0.9 constant_dynamic-slice_fusion
  152.8 1.2 convolution_bitcast_fusion
  154.0 3.3 copy.71
  157.4 1.3 dynamic-slice.4
  160.3 1045.6 %all-reduce.7.cloned.1.call-done = f32[128,2,2,1280]{3,2,1,0:T(2,128)} async-done(((f32[128,2,2,1280]{3,2,1,0:T(2,128)}), f32[128,2,2,1280]{3,2,1,0:T(2,128)}) %all-reduce.7.cloned.1.call-update) | async-done | bytes 2621456
  1205.9 1.0 dynamic-slice_reduce_fusion
  1207.0 1.1 fusion.19
  1208.2 1.1 fusion.17
  1209.3 1.1 fusion.15
  1210.4 1.1 fusion.13
  1213.9 145.5 %psum.7 = f32[32,32]{0,1:T(8,128)S(1)} all-reduce(f32[32,32]{0,1:T(8,128)S(1)} %convolution_bitcast_fusion.8), channel_id=1, replica_groups=mesh['row'=64,'col'=8] {'row','col'}, use_global_device_ids=true, to_apply=%region_3.4 | all-reduce | flops 1024 | bytes 8192 | tf_op jit(solution)/shard_map/psum | solution.py:99
  1359.4 0.7 copy.85
  1360.7 1.7 add_multiply_fusion
  1362.4 1.9 mul.549
  1364.9 0.9 pad_maximum_fusion
  1365.8 2.1 fusion.2
  1368.1 45.4 %all_gather.7 = bf16[4,2,64,5,32]{4,2,1,3,0:T(8,128)(2,1)S(1)} all-gather(bf16[4,2,8,5,32]{4,2,1,3,0:T(8,128)(2,1)S(1)} %copy.75), channel_id=1, replica_groups=mesh['row'=64,'col'=8] {'col'}, dimensions={2}, use_global_device_ids=true | all-gather | bytes 184320 | tf_op jit(solution)/shard_map/all_gather | solution.py:145
  1413.4 0.7 convolution_bitcast_fusion.4
  1414.1 1.8 convolution_bitcast_fusion.7
  1416.0 1.7 copy.77
  1417.7 1.4 copy.79
  1419.1 1.5 fusion
  1421.1 1.4 convert_element_type.163
  (60 shorter events, 7.6 us)
Async XLA Ops:
  7.2 1412.0 %copy-start = (bf16[32,32]{1,0:T(8,128)(2,1)S(1)}, bf16[32,32]{1,0:T(8,128)(2,1)}, u32[]{:S(2)}) copy-start(bf16[32,32]{1,0:T(8,128)(2,1)} %param.9) | copy-start | bytes 6148
  7.2 143.4 %all-reduce.9.cloned.1.call-start = ((), (), s32[]{:S(2)}) async-start(), calls=%async_computation.2 | async-start | bytes 2621440
  10.6 1.9 copy-start.1
  15.2 1190.7 %all-reduce.7.cloned.1.call-start = ((), (), s32[]{:S(2)}) async-start(), calls=%async_computation.1 | async-start | bytes 5242880
  157.3 1.4 copy-start.2
  157.4 1208.4 %all-gather.2.cloned.1.call-start = ((), (), s32[]{:S(2)}) async-start(), calls=%async_computation | async-start | bytes 1331200 | tf_op jit(solution)/shard_map/all_gather | solution.py:139
Sparse Core Ops, SparseCore 0:
  15.3 135.2 all-reduce.8
  157.5 1048.3 all-reduce.6
  1212.6 139.5 all-gather.1
where the time goes:
time: 1430 us
  waiting for transfers between devices  1180 us (83%)
  blocking collectives  191 us (13%)
  local copies, waits for them, and re-layouts  25.2 us (2%)
  between operations  15.4 us (1%)
  matrix products  14.9 us (1%)
    unnamed x5, waiting for transfers between devices  1180 us
    psum x1, blocking collectives, local(): bypass_total = lax.psum(local_bypass, ('row', 'col'))  146 us
    all_gather x1, blocking collectives, local(): lax.all_gather(rows_view.astype(jnp.bfloat16), 'col', axis=2, tiled=True)  45.4 us
  transfers between devices with their start and end apart: 3, of which 2 were waited for; matrix products, arithmetic and copies ran while one was open for 1% of the time, Pallas kernels for 0%

commit v1 on v0

--- a/solution.py
+++ b/solution.py
@@ -96,7 +96,8 @@
     local_bypass = jnp.einsum(
         "nc,nd->cd", flat_inputs, flat_grad, preferred_element_type=jnp.float32
     )
-    bypass_total = lax.psum(local_bypass, ("row", "col"))
+    compute_files = lambda matrix: lax.all_gather(matrix, ("row", "col")).sum(axis=0)
+    bypass_total = compute_files(local_bypass)
     grad_bypass = bypass_total * (1.0 / math.sqrt(float(total_x * total_y * step_count)))
     forward_t = time_forward(step_count, time_modes)
     col_table = phase_table(counting(col_modes), col_start + counting(col_count), total_y, -1.0)

time: 1430 us -> 1800 us (1.26)
  the two profiles are of different devices: /device:TPU:4 before, /device:TPU:2 now
where the time goes in v1:
time: 1800 us; the launch traced here: 1790 us
  waiting for transfers between devices  1680 us (93%)
  blocking collectives  45.4 us (3%)
  local copies, waits for them, and re-layouts  25.9 us (1%)
    unnamed x6, waiting for transfers between devices  1180 us
    all_gather x1, waiting for transfers between devices, local(): lax.all_gather(matrix, ('row', 'col')).sum(axis=0)  400 us
    all_gather x1, waiting for transfers between devices, local(): mode_piece = lax.all_gather(flat_back, 'row', axis=0, tiled=True)  105 us
    all_gather x1, blocking collectives, local(): lax.all_gather(rows_view.astype(jnp.bfloat16), 'col', axis=2, tiled=True)  45.4 us
  transfers between devices with their start and end apart: 4, of which 4 were waited for; matrix products, arithmetic and copies ran while one was open for 1% of the time, Pallas kernels for 0%

profile of v1, /device:TPU:2, one launch (start us, length us, event | category | flops | bytes accessed | tf_op | source)
XLA Modules:
  0.0 1794.6 jit_solution(10919044804261258862)
XLA Ops:
  8.3 1.1 copy.63
  9.4 1.1 copy.64
  11.4 0.7 fusion.7
  12.2 1.2 copy.67
  14.1 0.7 fusion.8
  14.8 1.2 copy.61
  16.1 1.3 dynamic-slice
  18.2 133.5 %all-reduce.9.cloned.1.call-done = (bf16[4,2,64,5,32]{4,0,3,1,2:T(4,128)(2,1)}, bf16[4,2,64,5,32]{4,0,3,1,2:T(4,128)(2,1)}) async-done(((bf16[4,2,64,5,32]{4,0,3,1,2:T(4,128)(2,1)}, bf16[4,2,64,5,32]{4,0,3,1,2:T(4,128)(2,1)}), (bf16[4,2,64,5,32]{4,0,3,1,2:T(4,128)(2,1)}, bf16[4,2,64,5,32]{4,0,3,1,2:T(4,128)(2,1)})) %all-reduce.9.cloned.1.call-update) | async-done | bytes 327696
  151.7 0.9 constant_dynamic-slice_fusion.1
  152.8 0.9 constant_dynamic-slice_fusion
  153.9 1.2 convolution_bitcast_fusion
  155.1 3.3 copy.71
  160.9 1.3 dynamic-slice.4
  163.7 1045.1 %all-reduce.7.cloned.1.call-done = f32[128,2,2,1280]{3,2,1,0:T(2,128)} async-done(((f32[128,2,2,1280]{3,2,1,0:T(2,128)}), f32[128,2,2,1280]{3,2,1,0:T(2,128)}) %all-reduce.7.cloned.1.call-update) | async-done | bytes 2621456
  1208.8 1.0 dynamic-slice_reduce_fusion
  1209.9 1.1 fusion.19
  1211.0 1.1 fusion.15
  1212.3 1.1 fusion.17
  1213.4 1.1 fusion.13
  1215.9 1.7 add_multiply_fusion
  1217.6 1.9 mul.549
  1220.1 0.9 pad_maximum_fusion
  1221.0 399.5 %all-gather.6.cloned.1.call-done = f32[16384,32]{1,0:T(8,128)} async-done(((f32[32,32]{1,0:T(8,128)}), f32[16384,32]{1,0:T(8,128)}) %all-gather.6.cloned.1.call-update) | async-done | bytes 2097168 | tf_op jit(solution)/shard_map/all_gather | solution.py:99
  1620.5 4.0 reduce_sum.9
  1625.3 105.1 %all-gather.4.cloned.1.call-done = f32[128,2,1280]{2,1,0:T(2,128)} async-done(((f32[2,2,1280]{2,1,0:T(2,128)}), f32[128,2,1280]{2,1,0:T(2,128)}) %all-gather.4.cloned.1.call-update) | async-done | bytes 1310736 | tf_op jit(solution)/shard_map/all_gather | solution.py:140
  1730.3 2.1 fusion.2
  1732.6 45.4 %all_gather.13 = bf16[4,2,64,5,32]{4,2,1,3,0:T(8,128)(2,1)S(1)} all-gather(bf16[4,2,8,5,32]{4,2,1,3,0:T(8,128)(2,1)S(1)} %copy.75), channel_id=1, replica_groups=mesh['row'=64,'col'=8] {'col'}, dimensions={2}, use_global_device_ids=true | all-gather | bytes 184320 | tf_op jit(solution)/shard_map/all_gather | solution.py:146
  1778.8 1.8 convolution_bitcast_fusion.7
  1780.6 1.7 copy.77
  1782.4 1.4 copy.79
  1783.7 1.5 fusion
  1785.7 1.4 convert_element_type.163
  (65 shorter events, 10.0 us)
Async XLA Ops:
  8.0 1775.7 %copy-start = (bf16[32,32]{1,0:T(8,128)(2,1)S(1)}, bf16[32,32]{1,0:T(8,128)(2,1)}, u32[]{:S(2)}) copy-start(bf16[32,32]{1,0:T(8,128)(2,1)} %param.9) | copy-start | bytes 6148
  8.0 143.6 %all-reduce.9.cloned.1.call-start = ((), (), s32[]{:S(2)}) async-start(), calls=%async_computation.3 | async-start | bytes 2621440
  11.4 1.9 copy-start.1
  16.0 1192.8 %all-reduce.7.cloned.1.call-start = ((), (), s32[]{:S(2)}) async-start(), calls=%async_computation.2 | async-start | bytes 5242880
  158.4 1462.1 %all-gather.6.cloned.1.call-start = ((), (), s32[]{:S(2)}) async-start(), calls=%async_computation.1 | async-start | bytes 8404992 | tf_op jit(solution)/shard_map/all_gather | solution.py:99
  159.5 2.7 copy-start.2
  160.7 1569.7 %all-gather.4.cloned.1.call-start = ((), (), s32[]{:S(2)}) async-start(), calls=%async_computation | async-start | bytes 1331200 | tf_op jit(solution)/shard_map/all_gather | solution.py:140
Sparse Core Ops, SparseCore 0:
  16.1 135.4 all-reduce.8
  158.5 1050.2 all-reduce.6
Sparse Core Ops, SparseCore 1:
  161.7 1458.8 all-gather.5
  1626.1 104.2 all-gather.3
